TPU v7x, 32 devices: a whole 2x2x4 slice. The times are simulated.
32 devices in a mesh: shard: 8 (over y, x, core), rep: 4 (over z).
Axes of the slice: x: 2, y: 2, z: 4, core: 2. Of those that a mesh axis runs over, the one named last changes fastest.
Arguments:
- latents: bfloat16 [32, 8, 2, 8, 1280], P(('shard', 'rep')), may hold values from -6 to 6
- depth_taps: bfloat16 [9, 1280], P(None, 'shard'), may hold values from -2 to 2
- time_taps: bfloat16 [3, 160, 1280], P(None, None, 'shard'), may hold values from -0.25 to 0.25
- cotangent: bfloat16 [32, 8, 2, 8, 1280], P(('shard', 'rep')), may hold values from -12 to 12, as said below
Outputs:
- block_out: bfloat16 [32, 8, 2, 8, 1280], P(('shard', 'rep'))
- input_grad: bfloat16 [32, 8, 2, 8, 1280], P(('shard', 'rep'))
- depth_grad: float32 [9, 1280], P(None, 'shard')
- time_grad: float32 [3, 160, 1280], P(None, None, 'shard')
Inputs may be any that keep to these rules, and one draw needn't show every extreme that they name: Each clip's cotangent has a scale of its own.
All inputs are finite; a program needn't handle non-finite values.
Results may differ from a plain program's by a relative error of at most 0.003.
Values may be sent and summed in bfloat16 or wider, within the bound.
A program may use at most 64 MiB of HBM per device.

v0:
```python
import functools

import jax
import jax.numpy as jnp
from jax import lax
from jax.experimental import pallas as pl
from jax.experimental.pallas import tpu as pltpu
from jax.sharding import PartitionSpec as P

GROUPS = 8


def moved(field, offset):
    if offset == 0:
        return field
    filler = jnp.zeros((field.shape[0], abs(offset)), field.dtype)
    if offset > 0:
        return jnp.concatenate([field[:, offset:], filler], 1)
    return jnp.concatenate([filler, field[:, :offset]], 1)


def inside(frames, height, breadth, frame_off, row_off, col_off):
    places = jnp.arange(frames * height * breadth, dtype=jnp.int32)
    frame_at = places // (height * breadth) + frame_off
    row_at = places // breadth % height + row_off
    col_at = places % breadth + col_off
    valid = (frame_at >= 0) & (frame_at < frames) & (row_at >= 0) & (row_at < height)
    valid = valid & (col_at >= 0) & (col_at < breadth)
    return valid[None, :]


def clip_pass(latent, cotan, depth_full, time_full):
    frames, height, breadth, chans = latent.shape
    plane = height * breadth
    count = frames * plane
    width = chans // GROUPS
    x_cols = latent.reshape(count, chans).T
    dy_cols = cotan.reshape(count, chans).T
    wdf = depth_full.astype(jnp.float32)
    spatial = jnp.zeros((chans, count), jnp.float32)
    for tap in range(9):
        row_off = tap // 3 - 1
        col_off = tap % 3 - 1
        offset = row_off * breadth + col_off
        shifted = jnp.where(
            inside(frames, height, breadth, 0, row_off, col_off), moved(x_cols, offset), 0
        )
        spatial = spatial + shifted * wdf[tap][:, None]
    inv_rms = lax.rsqrt(jnp.mean(spatial * spatial, 0, keepdims=True) + 1e-05)
    normed = spatial * inv_rms
    activated = jax.nn.silu(normed).astype(jnp.bfloat16)
    act_parts = []
    dy_parts = []
    for step in range(3):
        act_off = step - 1
        act_shift = jnp.where(
            inside(frames, height, breadth, act_off, 0, 0), moved(activated, act_off * plane), 0
        )
        act_parts.append(act_shift.reshape(GROUPS, width, count))
        dy_off = 1 - step
        dy_shift = jnp.where(
            inside(frames, height, breadth, dy_off, 0, 0), moved(dy_cols, dy_off * plane), 0
        )
        dy_parts.append(dy_shift.reshape(GROUPS, width, count))
    act_stack = jnp.concatenate(act_parts, 1)
    dy_stack = jnp.concatenate(dy_parts, 1)
    grouped = time_full.reshape(3, width, GROUPS, width)
    fwd_weight = grouped.transpose(2, 3, 0, 1).reshape(GROUPS, width, 3 * width)
    back_weight = grouped.transpose(2, 1, 0, 3).reshape(GROUPS, width, 3 * width)
    temporal = jnp.einsum(
        "goc,gcr->gor", fwd_weight, act_stack, preferred_element_type=jnp.float32
    ).reshape(chans, count)
    block_out = (x_cols.astype(jnp.float32) + temporal).astype(jnp.bfloat16)
    act_grad = jnp.einsum(
        "gic,gcr->gir", back_weight, dy_stack, preferred_element_type=jnp.float32
    ).reshape(chans, count)
    dy_group = dy_cols.reshape(GROUPS, width, count)
    time_term = jnp.einsum("gcr,gor->goc", act_stack, dy_group, preferred_element_type=jnp.float32)
    time_term = (
        time_term.reshape(GROUPS, width, 3, width).transpose(2, 3, 0, 1).reshape(3, width, chans)
    )
    sig = jax.nn.sigmoid(normed)
    norm_grad = act_grad * sig * (1.0 + normed * (1.0 - sig))
    spatial_grad = inv_rms * (norm_grad - normed * jnp.mean(norm_grad * normed, 0, keepdims=True))
    input_grad = dy_cols.astype(jnp.float32)
    depth_terms = []
    for tap in range(9):
        row_off = tap // 3 - 1
        col_off = tap % 3 - 1
        offset = row_off * breadth + col_off
        back_shift = jnp.where(
            inside(frames, height, breadth, 0, -row_off, -col_off),
            moved(spatial_grad, -offset),
            0.0,
        )
        input_grad = input_grad + back_shift * wdf[tap][:, None]
        shifted = jnp.where(
            inside(frames, height, breadth, 0, row_off, col_off), moved(x_cols, offset), 0
        )
        depth_terms.append(jnp.sum(shifted.astype(jnp.float32) * spatial_grad, axis=1))
    depth_term = jnp.stack(depth_terms)
    out_rows = block_out.T.reshape(latent.shape)
    grad_rows = input_grad.astype(jnp.bfloat16).T.reshape(latent.shape)
    return (out_rows, grad_rows, depth_term, time_term)


def per_device(latents, depth_taps, time_taps, cotangent):
    depth_full, time_full = (
        lax.all_gather(depth_taps, "shard", axis=1, tiled=True),
        lax.all_gather(time_taps, "shard", axis=2, tiled=True),
    )
    block_out, input_grad, depth_term, time_term = clip_pass(
        latents[0], cotangent[0], depth_full, time_full
    )
    scale = jnp.float32(1.0 / (lax.axis_size("shard") * lax.axis_size("rep")))
    depth_term = depth_term * scale
    time_term = time_term * scale
    time_part, depth_part = (
        lax.psum_scatter(time_term, "shard", scatter_dimension=2, tiled=True),
        lax.psum_scatter(depth_term, "shard", scatter_dimension=1, tiled=True),
    )
    time_grad, depth_grad = lax.psum((time_part, depth_part), "rep")
    return (block_out[None], input_grad[None], depth_grad, time_grad)


MESH = pl.DeviceIdType.MESH
LANES = 128


def window(group):
    return 128 * (group + group // 4)


def fused_kernel(
    n, reps, scale,
    x_hbm, dtaps_hbm, ttaps_hbm, dy_hbm,
    out_hbm, gin_hbm, dgrad_ref, tgrad_ref,
    out_ref, gin_ref, out_sem,
    x_ref, dtaps_ref, ttaps_ref, dy_ref, in_sem,
    sp, slope, ag, acc, act_pad, cot_pad, act_t, cot_t, act_all, cot_all, cot_sh,
    w_mine, w_in, w_all, d_mine, d_all, d_full,
    tg, tg_send, tg_recv, tg_out, dg, dg_send, dg_recv, dz_mine, dz_recv,
    d_ss, d_rs, c_ss, c_rs, a_ss, a_rs, w_ss, w_rs, f_ss, f_rs,
    r_ss, r_rs, g_ss, g_rs, p_ss, p_rs, q_ss, q_rs,
):
    frames, height, breadth, chans = sp.shape
    plane = height * breadth
    count = frames * plane
    width = chans // n
    tiles = chans // LANES
    me = lax.axis_index("shard")
    z = lax.axis_index("rep")
    sib = me + 1 - 2 * lax.rem(me, 2)
    shift = 32 * lax.rem(me, 4)

    def ahead(r):
        return lax.rem(me + r, n)

    def behind(r):
        return lax.rem(me + n - r, n)

    def zahead(r):
        return lax.rem(z + r, reps)

    def zbehind(r):
        return lax.rem(z + reps - r, reps)

    def remote(src, dst, ss, rs, **where):
        return pltpu.make_async_remote_copy(
            src_ref=src, dst_ref=dst, send_sem=ss, recv_sem=rs,
            device_id=where, device_id_type=MESH,
        )

    loads = [
        pltpu.make_async_copy(src, dst, in_sem.at[i])
        for i, (src, dst) in enumerate((
            (dtaps_hbm, dtaps_ref), (dy_hbm, dy_ref), (ttaps_hbm, ttaps_ref), (x_hbm, x_ref),
        ))
    ]
    for load in loads:
        load.start()
    barrier = pltpu.get_barrier_semaphore()
    for r in range(1, n):
        pl.semaphore_signal(barrier, inc=1, device_id={"shard": ahead(r)}, device_id_type=MESH)
    for r in range(1, reps):
        pl.semaphore_signal(barrier, inc=1, device_id={"rep": zahead(r)}, device_id_type=MESH)

    edge = jnp.zeros((plane, chans), jnp.bfloat16)
    act_pad[0:plane, :] = edge
    act_pad[count + plane:count + 2 * plane, :] = edge
    cot_pad[0:plane, :] = edge
    cot_pad[count + plane:count + 2 * plane, :] = edge
    for g in range(n):
        low = 32 * (g % 4)
        for k in range(3):
            if low > 0:
                w_all[g, k, 0:low, :] = jnp.zeros((low, 256), jnp.bfloat16)
            if low < 96:
                w_all[g, k, low + width:256, :] = jnp.zeros((96 - low, 256), jnp.bfloat16)
    ag[...] = jnp.zeros(ag.shape, jnp.float32)
    dg[...] = jnp.zeros(dg.shape, jnp.float32)
    cot_sh[3 * width:512, :] = jnp.zeros((512 - 3 * width, n * count), jnp.bfloat16)

    place = (
        lax.broadcasted_iota(jnp.int32, (width, 256), 1)
        == lax.broadcasted_iota(jnp.int32, (width, 256), 0) + shift
    ).astype(jnp.float32).astype(jnp.bfloat16)
    loads[0].wait()
    taps = jnp.concatenate(
        [dtaps_ref[...].astype(jnp.float32), jnp.zeros((7, width), jnp.float32)], axis=0
    ).astype(jnp.bfloat16)
    d_mine[...] = jnp.dot(taps, place, preferred_element_type=jnp.float32).astype(jnp.bfloat16)

    def cot_tile(t, carry):
        cols = pl.ds(pl.multiple_of(t * LANES, LANES), LANES)
        tile = dy_ref[0, :, :, :, cols].astype(jnp.float32).reshape(count, LANES)
        cot_pad[pl.ds(plane, count), cols] = tile.astype(jnp.bfloat16)
        cot_t[pl.ds(pl.multiple_of(t * LANES, LANES), LANES), :] = tile.T.astype(jnp.bfloat16)
        return carry

    loads[1].wait()
    lax.fori_loop(0, tiles, cot_tile, 0, unroll=2)
    loads[2].wait()
    row = lax.broadcasted_iota(jnp.int32, (width, LANES), 0)
    lane = lax.broadcasted_iota(jnp.int32, (width, LANES), 1)
    first = jnp.where((row < LANES) & (lax.rem(row + shift, LANES) == lane), 1.0, 0.0)
    first = first.astype(jnp.bfloat16)
    rest = jnp.zeros((width, LANES), jnp.float32)
    for k in range(3):
        spot = lax.rem(row + shift + 32 * k, LANES) == lane
        last = jnp.where((row >= LANES) & spot, 1.0, 0.0).astype(jnp.bfloat16)
        tap = ttaps_ref[k]
        w_mine[k] = jnp.dot(tap, first, preferred_element_type=jnp.float32).astype(jnp.bfloat16)
        rest = rest + jnp.dot(tap, last, preferred_element_type=jnp.float32)
    w_mine[3] = rest.astype(jnp.bfloat16)
    pl.semaphore_wait(barrier, n - 1 + reps - 1)

    d_copies = [
        remote(d_mine, d_all.at[me], d_ss.at[r - 1], d_rs.at[r - 1], shard=ahead(r))
        for r in range(1, n)
    ]
    for copy in d_copies:
        copy.start()

    def slab(p):
        return pl.ds(pl.multiple_of(p * width, 32), width)

    def lane_block(p):
        return pl.ds(pl.multiple_of(p * count, LANES), count)

    c_copies = [
        remote(
            cot_t.at[slab(ahead(r)), :], cot_all.at[:, lane_block(me)],
            c_ss.at[r - 1], c_rs.at[r - 1], shard=ahead(r),
        )
        for r in range(1, n)
    ]
    for copy in c_copies:
        copy.start()

    hops = list(range(2, n, 2))

    def w_send(c):
        cut = pl.ds(2 * c, 2)
        copies = [
            remote(w_mine.at[cut], w_in.at[me, cut], w_ss.at[c, i], w_rs.at[c, i], shard=ahead(r))
            for i, r in enumerate(hops)
        ]
        copies.append(remote(
            w_mine.at[cut], w_in.at[me, cut], w_ss.at[c, n // 2 - 1], w_rs.at[c, n // 2 - 1],
            shard=sib,
        ))
        for copy in copies:
            copy.start()
        return copies

    f_copies = []

    def w_pass(c):
        cut = pl.ds(2 * c, 2)
        for i, r in enumerate(hops):
            there = w_in.at[behind(r), cut]
            remote(w_mine.at[cut], there, w_ss.at[c, i], w_rs.at[c, i], shard=ahead(r)).wait_recv()
            f_copies.append(remote(there, there, f_ss.at[c, i], f_rs.at[c, i], shard=sib))
            f_copies[-1].start()

    w_copies = w_send(0)
    d_all[me] = d_mine[...]
    w_in[me] = w_mine[...]
    cot_all[:, lane_block(me)] = cot_t[slab(me), :]
    for r in range(1, n):
        remote(
            d_mine, d_all.at[behind(r)], d_ss.at[r - 1], d_rs.at[r - 1], shard=ahead(r)
        ).wait_recv()
    d_full[...] = jnp.zeros(d_full.shape, jnp.float32)
    for g in range(n):
        lo = window(g)
        d_full[:, lo:lo + 256] = d_full[:, lo:lo + 256] + d_all[g].astype(jnp.float32)

    column = lax.broadcasted_iota(jnp.int32, (frames, height, breadth, LANES), 2)

    def from_left(v):
        rolled = pltpu.roll(v.reshape(frames * height, breadth, LANES), 1, 1)
        return jnp.where(column == 0, 0.0, rolled.reshape(v.shape))

    def from_right(v):
        rolled = pltpu.roll(v.reshape(frames * height, breadth, LANES), breadth - 1, 1)
        return jnp.where(column == breadth - 1, 0.0, rolled.reshape(v.shape))

    def cols_of(t):
        return pl.ds(pl.multiple_of(t * LANES, LANES), LANES)

    def spatial_tile(t, carry):
        cols = cols_of(t)
        x = x_ref[0, :, :, :, cols].astype(jnp.float32)
        d = [d_full[k:k + 1, cols].reshape(1, 1, LANES) for k in range(9)]
        xs = [from_left(x), x, from_right(x)]
        top = sum(xs[j][:, 0] * d[3 + j] + xs[j][:, 1] * d[6 + j] for j in range(3))
        low = sum(xs[j][:, 0] * d[j] + xs[j][:, 1] * d[3 + j] for j in range(3))
        sp[:, 0, :, cols] = top
        sp[:, 1, :, cols] = low
        return (carry[0] + top * top, carry[1] + low * low)

    zero = jnp.zeros((frames, breadth, LANES), jnp.float32)
    loads[3].wait()
    squares = lax.fori_loop(0, tiles, spatial_tile, (zero, zero), unroll=2)
    inv = [
        lax.rsqrt(jnp.sum(s, axis=-1, keepdims=True) * (1.0 / chans) + 1e-05) for s in squares
    ]
    inv_rms = jnp.concatenate([v[:, None] for v in inv], axis=1)

    def act_tile(t, carry):
        cols = cols_of(t)
        normed = sp[:, :, :, cols] * inv_rms
        sig = jax.nn.sigmoid(normed)
        sp[:, :, :, cols] = normed
        slope[:, :, :, cols] = sig * (1.0 + normed * (1.0 - sig))
        tile = (normed * sig).reshape(count, LANES)
        act_pad[pl.ds(plane, count), cols] = tile.astype(jnp.bfloat16)
        act_t[cols, :] = tile.T.astype(jnp.bfloat16)
        return carry

    lax.fori_loop(0, tiles, act_tile, 0, unroll=2)

    a_copies = [
        remote(
            act_t.at[slab(ahead(r)), :], act_all.at[:, lane_block(me)],
            a_ss.at[r - 1], a_rs.at[r - 1], shard=ahead(r),
        )
        for r in range(1, n)
    ]
    for copy in a_copies:
        copy.start()
    w_copies += w_send(1)
    act_all[:, lane_block(me)] = act_t[slab(me), :]

    for r in range(1, n):
        remote(
            cot_t.at[slab(me), :], cot_all.at[:, lane_block(behind(r))],
            c_ss.at[r - 1], c_rs.at[r - 1], shard=ahead(r),
        ).wait_recv()
    src = lax.broadcasted_iota(jnp.int32, (count, 2 * count), 0)
    dst = lax.broadcasted_iota(jnp.int32, (count, 2 * count), 1)
    target = dst + jnp.where(dst < count, plane, -plane - count)
    mover = jnp.where(src == target, 1.0, 0.0).astype(jnp.bfloat16)
    for c in range(n):
        lanes = slice(c * count, (c + 1) * count)
        moved_cot = jnp.dot(cot_all[:, lanes], mover, preferred_element_type=jnp.float32)
        cot_sh[0:width, lanes] = moved_cot[:, :count].astype(jnp.bfloat16)
        cot_sh[width:2 * width, lanes] = cot_all[:, lanes]
        cot_sh[2 * width:3 * width, lanes] = moved_cot[:, count:].astype(jnp.bfloat16)
    for r in range(1, n):
        remote(
            act_t.at[slab(me), :], act_all.at[:, lane_block(behind(r))],
            a_ss.at[r - 1], a_rs.at[r - 1], shard=ahead(r),
        ).wait_recv()
    nt = (((1,), (1,)), ((), ()))
    part = width // reps
    product = lax.dot_general(act_all[...], cot_sh[...], nt, preferred_element_type=jnp.float32)
    tg[...] = product.reshape(reps, part, 512)
    tg_send[...] = tg[...].astype(jnp.bfloat16)
    r_copies = [
        remote(
            tg_send.at[zahead(r)], tg_recv.at[r - 1], r_ss.at[r - 1], r_rs.at[r - 1],
            rep=zahead(r),
        )
        for r in range(1, reps)
    ]
    for copy in r_copies:
        copy.start()

    nn = (((1,), (0,)), ((), ()))
    lane = lax.broadcasted_iota(jnp.int32, (width, LANES), 1)

    def mask(hit):
        return jnp.where(hit, 1.0, 0.0).astype(jnp.bfloat16)

    def group_grad(p):
        off = 32 * lax.rem(p, 4)
        rows = pl.ds(pl.multiple_of(off, 32), width)
        near, far = mask(lane >= off), mask(lane < off)
        tail = mask((lane >= off) & (lane < off + 32))
        rest = w_in[p, 3].astype(jnp.float32)
        for k in range(3):
            turned = rest if k == 0 else pltpu.roll(rest, LANES - 32 * k, 1)
            main = w_in[p, k]
            w_all[p, k, rows, 0:LANES] = main * near
            w_all[p, k, rows, LANES:256] = main * far + turned.astype(jnp.bfloat16) * tail
        lanes = pl.ds(pl.multiple_of(window(p), LANES), 256)
        term = sum(
            lax.dot_general(
                cot_pad[plane * (2 - k):plane * (2 - k) + count, lanes], w_all[p, k], nt,
                preferred_element_type=jnp.float32,
            )
            for k in range(3)
        )
        ag[:, lanes] = ag[:, lanes] + term

    w_pass(0)
    group_grad(me)
    w_pass(1)

    for c in range(2):
        cut = pl.ds(2 * c, 2)
        remote(w_mine.at[cut], w_in.at[sib, cut], w_ss.at[c, n // 2 - 1], w_rs.at[c, n // 2 - 1],
               shard=sib).wait_recv()
    group_grad(sib)
    for r in hops:
        group_grad(behind(r))
    for i, r in enumerate(hops):
        p = lax.rem(sib + n - r, n)
        for c in range(2):
            there = w_in.at[p, pl.ds(2 * c, 2)]
            remote(there, there, f_ss.at[c, i], f_rs.at[c, i], shard=sib).wait_recv()
        group_grad(p)

    def grouped(source, order, weight_dims, store):
        for g in range(n):
            lo = window(g)
            term = sum(
                lax.dot_general(
                    source[plane * order(k):plane * order(k) + count, lo:lo + 256],
                    w_all[g, k], weight_dims, preferred_element_type=jnp.float32,
                )
                for k in range(3)
            )
            if g % 4 == 0:
                store[:, lo:lo + 256] = term
            else:
                store[:, lo:lo + 128] = store[:, lo:lo + 128] + term[:, :128]
                store[:, lo + 128:lo + 256] = term[:, 128:]

    def norm_tile(t, carry):
        cols = cols_of(t)
        grad = ag[:, cols].reshape(frames, height, breadth, LANES) * slope[:, :, :, cols]
        ag[:, cols] = grad.reshape(count, LANES)
        return carry + grad * sp[:, :, :, cols]

    dots = lax.fori_loop(
        0, tiles, norm_tile, jnp.zeros((frames, height, breadth, LANES), jnp.float32), unroll=2)
    mean = jnp.sum(dots, axis=-1, keepdims=True) * (1.0 / chans)


    def depth_tile(t, carry):
        cols = cols_of(t)
        grad = ag[:, cols].reshape(frames, height, breadth, LANES)
        sg = inv_rms * (grad - sp[:, :, :, cols] * mean)
        ag[:, cols] = sg.reshape(count, LANES)
        gs = [from_right(sg), sg, from_left(sg)]
        x = x_ref[0, :, :, :, cols].astype(jnp.float32)
        x0, x1 = x[:, 0], x[:, 1]
        for j in range(3):
            g0, g1 = gs[j][:, 0], gs[j][:, 1]
            for i, term in enumerate((x0 * g1, x0 * g0 + x1 * g1, x1 * g0)):
                dg[3 * i + j:3 * i + j + 1, cols] = jnp.sum(
                    jnp.sum(term, axis=0), axis=0, keepdims=True
                )
        return carry

    lax.fori_loop(0, tiles, depth_tile, 0, unroll=2)

    def grad_tile(t, carry):
        cols = cols_of(t)
        sg = ag[:, cols].reshape(frames, height, breadth, LANES)
        d = [d_full[k:k + 1, cols].reshape(1, 1, LANES) for k in range(9)]
        gs = [from_right(sg), sg, from_left(sg)]
        top = dy_ref[0, :, 0, :, cols].astype(jnp.float32)
        low = dy_ref[0, :, 1, :, cols].astype(jnp.float32)
        for j in range(3):
            g0, g1 = gs[j][:, 0], gs[j][:, 1]
            top = top + g0 * d[3 + j] + g1 * d[j]
            low = low + g0 * d[6 + j] + g1 * d[3 + j]
        gin_ref[0, :, 0, :, cols] = top.astype(jnp.bfloat16)
        gin_ref[0, :, 1, :, cols] = low.astype(jnp.bfloat16)
        return carry

    def dwin(p):
        return pl.ds(pl.multiple_of(window(p), LANES), 256)

    dg_send[...] = dg[...].astype(jnp.bfloat16)
    p_copies = [
        remote(dg_send.at[:, dwin(ahead(r))], dg_recv.at[me], p_ss.at[r - 1], p_rs.at[r - 1],
               shard=ahead(r))
        for r in range(1, n)
    ]
    for copy in p_copies:
        copy.start()
    dg_recv[me] = dg_send[:, dwin(me)]

    for r in range(1, reps):
        r_copies[r - 1].wait_recv()
    total = tg[z]
    for r in range(1, reps):
        total = total + tg_recv[r - 1].astype(jnp.float32)
    tg_out[z] = (total * scale).astype(jnp.bfloat16)
    g_copies = [
        remote(tg_out.at[z], tg_out.at[z], g_ss.at[r - 1], g_rs.at[r - 1], rep=zahead(r))
        for r in range(1, reps)
    ]
    for copy in g_copies:
        copy.start()

    grouped(act_pad, lambda k: k, nn, acc)

    def depth_first():
        for r in range(1, n):
            remote(dg_send.at[:, dwin(me)], dg_recv.at[behind(r)], p_ss.at[r - 1], p_rs.at[r - 1],
                   shard=ahead(r)).wait_recv()
        total = dg_recv[0].astype(jnp.float32)
        for p in range(1, n):
            total = total + dg_recv[p].astype(jnp.float32)
        dz_mine[...] = total.astype(jnp.bfloat16)
        copies = [
            remote(dz_mine, dz_recv.at[z], q_ss.at[r - 1], q_rs.at[r - 1], rep=zahead(r))
            for r in range(1, reps)
        ]
        for copy in copies:
            copy.start()
        dz_recv[z] = dz_mine[...]
        return copies

    q_copies = depth_first()
    lax.fori_loop(0, tiles, grad_tile, 0, unroll=2)
    gin_store = pltpu.make_async_copy(gin_ref, gin_hbm, out_sem.at[0])
    gin_store.start()

    def out_tile(t, carry):
        cols = cols_of(t)
        x = x_ref[0, :, :, :, cols].astype(jnp.float32)
        y = x + acc[:, cols].reshape(frames, height, breadth, LANES)
        out_ref[0, :, :, :, cols] = y.astype(jnp.bfloat16)
        return carry

    lax.fori_loop(0, tiles, out_tile, 0, unroll=2)
    out_store = pltpu.make_async_copy(out_ref, out_hbm, out_sem.at[1])
    out_store.start()

    for r in range(1, reps):
        remote(tg_out.at[z], tg_out.at[zbehind(r)], g_ss.at[r - 1], g_rs.at[r - 1],
               rep=zahead(r)).wait_recv()
    grads = tg_out[...].astype(jnp.float32).reshape(width, 512)
    for k in range(3):
        tgrad_ref[k] = grads[:, k * width:(k + 1) * width]

    for r in range(1, reps):
        remote(dz_mine, dz_recv.at[zbehind(r)], q_ss.at[r - 1], q_rs.at[r - 1],
               rep=zahead(r)).wait_recv()
    whole = dz_recv[0].astype(jnp.float32)
    for r in range(1, reps):
        whole = whole + dz_recv[r].astype(jnp.float32)
    whole = pltpu.roll(whole * scale, lax.rem(256 - shift, 256), 1)
    dgrad_ref[...] = whole[0:9, 0:width]

    gin_store.wait()
    out_store.wait()
    for copies in (d_copies, c_copies, a_copies, w_copies, f_copies, r_copies, g_copies,
                   p_copies, q_copies):
        for copy in copies:
            copy.wait_send()


def fused_device(latents, depth_taps, time_taps, cotangent):
    n, reps = lax.axis_size("shard"), lax.axis_size("rep")
    _, frames, height, breadth, chans = latents.shape
    count = frames * height * breadth
    padded = count + 2 * height * breadth
    width = chans // n
    bf, f32 = jnp.bfloat16, jnp.float32
    dma = pltpu.SemaphoreType.DMA
    part = width // reps
    vmem = pl.BlockSpec(memory_space=pltpu.VMEM)
    return pl.pallas_call(
        functools.partial(fused_kernel, n, reps, 1.0 / (n * reps)),
        out_shape=(
            jax.ShapeDtypeStruct(latents.shape, bf),
            jax.ShapeDtypeStruct(latents.shape, bf),
            jax.ShapeDtypeStruct((9, width), f32),
            jax.ShapeDtypeStruct((3, width, width), f32),
        ),
        in_specs=[pl.BlockSpec(memory_space=pltpu.HBM)] * 4,
        out_specs=[pl.BlockSpec(memory_space=pltpu.HBM)] * 2 + [vmem] * 2,
        scratch_shapes=[
            pltpu.VMEM(latents.shape, bf),
            pltpu.VMEM(latents.shape, bf),
            dma((2,)),
            pltpu.VMEM(latents.shape, bf),
            pltpu.VMEM(depth_taps.shape, bf),
            pltpu.VMEM(time_taps.shape, bf),
            pltpu.VMEM(cotangent.shape, bf),
            dma((4,)),
            pltpu.VMEM((frames, height, breadth, chans), f32),
            pltpu.VMEM((frames, height, breadth, chans), f32),
            pltpu.VMEM((count, chans), f32),
            pltpu.VMEM((count, chans), f32),
            pltpu.VMEM((padded, chans), bf),
            pltpu.VMEM((padded, chans), bf),
            pltpu.VMEM((chans, count), bf),
            pltpu.VMEM((chans, count), bf),
            pltpu.VMEM((width, n * count), bf),
            pltpu.VMEM((width, n * count), bf),
            pltpu.VMEM((512, n * count), bf),
            pltpu.VMEM((4, width, LANES), bf),
            pltpu.VMEM((n, 4, width, LANES), bf),
            pltpu.VMEM((n, 3, 256, 256), bf),
            pltpu.VMEM((16, 256), bf),
            pltpu.VMEM((n, 16, 256), bf),
            pltpu.VMEM((16, chans), f32),
            pltpu.VMEM((reps, part, 512), f32),
            pltpu.VMEM((reps, part, 512), bf),
            pltpu.VMEM((reps - 1, part, 512), bf),
            pltpu.VMEM((reps, part, 512), bf),
            pltpu.VMEM((16, chans), f32),
            pltpu.VMEM((16, chans), bf),
            pltpu.VMEM((n, 16, 256), bf),
            pltpu.VMEM((16, 256), bf),
            pltpu.VMEM((reps, 16, 256), bf),
            dma((n - 1,)), dma((n - 1,)),
            dma((n - 1,)), dma((n - 1,)),
            dma((n - 1,)), dma((n - 1,)),
            dma((2, n // 2)), dma((2, n // 2)),
            dma((2, n // 2 - 1)), dma((2, n // 2 - 1)),
            dma((reps - 1,)), dma((reps - 1,)),
            dma((reps - 1,)), dma((reps - 1,)),
            dma((n - 1,)), dma((n - 1,)),
            dma((reps - 1,)), dma((reps - 1,)),
        ],
        compiler_params=pltpu.CompilerParams(
            collective_id=0, has_side_effects=True, vmem_limit_bytes=63 * 1024 * 1024
        ),
    )(latents, depth_taps, time_taps, cotangent)


def solution(mesh):
    placed = (
        P(("shard", "rep"), None, None, None, None),
        P(None, "shard"),
        P(None, None, "shard"),
        P(("shard", "rep"), None, None, None, None),
    )
    shards, reps = mesh.shape["shard"], mesh.shape["rep"]
    fused = shards == GROUPS and reps in (2, 4)
    return jax.shard_map(
        fused_device if fused else per_device,
        mesh=mesh,
        in_specs=placed,
        out_specs=(
            P(("shard", "rep"), None, None, None, None),
            P(("shard", "rep"), None, None, None, None),
            P(None, "shard"),
            P(None, None, "shard"),
        ),
        check_vma=False,
    )
```

profile of v0, /device:TPU:0, one launch (start us, length us, event | category | flops | bytes accessed | tf_op | source)
XLA Modules:
  0.0 39.2 jit_solution(13353340293866987169)
XLA Ops:
  0.6 34.7 %shard_map.75 = (bf16[1,8,2,8,1280]{4,3,2,1,0:T(8,128)(2,1)}, bf16[1,8,2,8,1280]{4,3,2,1,0:T(8,128)(2,1)}, f32[9,160]{1,0:T(8,128)}, f32[3,160,160]{2,1,0:T(8,128)}) custom-call(bf16[1,8,2,8,1280]{4,3,2,1,0:T(8,128)(2,1)} %x_hbm.1, bf16[9,160]{1,0:T(8,128)(2,1)} %dtaps_hbm.1, bf16[3,160,160]{2,1,0:T(8,128)(2,1)} %ttaps_hbm.1, bf16[1,8,2,8,1280]{4,3,2,1,0:T(8,128)(2,1)} %dy_hbm.1), custom_call_target="tpu_custom_call" | custom-call | tf_op jit(solution)/shard_map/pallas_call | solution.py:592
  35.3 0.0 copy-start.1
  35.3 1.8 %copy.12 = bf16[1,8,2,8,1280]{4,3,2,1,0:T(8,128)(2,1)} copy(bf16[1,8,2,8,1280]{4,3,2,1,0:T(8,128)(2,1)} %get-tuple-element.8) | data formatting | bytes 655360
  37.1 0.0 copy-done.1
  37.1 0.0 copy-start.2
  37.1 0.0 copy-start
  37.1 0.7 %copy.13 = bf16[1,8,2,8,1280]{4,3,2,1,0:T(8,128)(2,1)} copy(bf16[1,8,2,8,1280]{4,3,2,1,0:T(8,128)(2,1)S(1)} %copy-done.1) | data formatting | bytes 655360
  37.8 0.0 copy-done.2
  37.8 0.6 %copy.14 = f32[9,160]{1,0:T(8,128)} copy(f32[9,160]{1,0:T(8,128)S(1)} %copy-done.2) | data formatting | bytes 11520
  38.5 0.0 copy-done
  38.5 0.8 %copy.15 = f32[3,160,160]{2,1,0:T(8,128)} copy(f32[3,160,160]{2,1,0:T(8,128)S(1)} %copy-done) | data formatting | bytes 614400
Async XLA Ops:
  35.3 1.8 %copy-start.1 = (bf16[1,8,2,8,1280]{4,3,2,1,0:T(8,128)(2,1)S(1)}, bf16[1,8,2,8,1280]{4,3,2,1,0:T(8,128)(2,1)}, u32[]{:S(2)}) copy-start(bf16[1,8,2,8,1280]{4,3,2,1,0:T(8,128)(2,1)} %get-tuple-element.9) | copy-start | bytes 983044
  37.1 0.7 %copy-start.2 = (f32[9,160]{1,0:T(8,128)S(1)}, f32[9,160]{1,0:T(8,128)}, u32[]{:S(2)}) copy-start(f32[9,160]{1,0:T(8,128)} %get-tuple-element.10) | copy-start | bytes 17284
  37.1 1.3 %copy-start = (f32[3,160,160]{2,1,0:T(8,128)S(1)}, f32[3,160,160]{2,1,0:T(8,128)}, u32[]{:S(2)}) copy-start(f32[3,160,160]{2,1,0:T(8,128)} %get-tuple-element.11) | copy-start | bytes 921604
where the time goes:
time: 39.5 us; the launch traced here: 39.2 us
  Pallas kernels  34.7 us (88%)
  local copies, waits for them, and re-layouts  3.88 us (10%)
  between operations  0.65 us (2%)
    pallas_call x1, Pallas kernels, fused_device(): pl.pallas_call(functools.partial(fused_kernel, n, reps, 1.0 / (n * reps))...  34.7 us
    unnamed x10, local copies, waits for them, and re-layouts  3.88 us

commit v1 on v0

--- a/solution.py
+++ b/solution.py
@@ -134,8 +134,7 @@
 def fused_kernel(
     n, reps, scale,
     x_hbm, dtaps_hbm, ttaps_hbm, dy_hbm,
-    out_hbm, gin_hbm, dgrad_ref, tgrad_ref,
-    out_ref, gin_ref, out_sem,
+    out_ref, gin_ref, dgrad_ref, tgrad_ref,
     x_ref, dtaps_ref, ttaps_ref, dy_ref, in_sem,
     sp, slope, ag, acc, act_pad, cot_pad, act_t, cot_t, act_all, cot_all, cot_sh,
     w_mine, w_in, w_all, d_mine, d_all, d_full,
@@ -541,8 +540,6 @@
 
     q_copies = depth_first()
     lax.fori_loop(0, tiles, grad_tile, 0, unroll=2)
-    gin_store = pltpu.make_async_copy(gin_ref, gin_hbm, out_sem.at[0])
-    gin_store.start()
 
     def out_tile(t, carry):
         cols = cols_of(t)
@@ -552,8 +549,6 @@
         return carry
 
     lax.fori_loop(0, tiles, out_tile, 0, unroll=2)
-    out_store = pltpu.make_async_copy(out_ref, out_hbm, out_sem.at[1])
-    out_store.start()
 
     for r in range(1, reps):
         remote(tg_out.at[z], tg_out.at[zbehind(r)], g_ss.at[r - 1], g_rs.at[r - 1],
@@ -571,8 +566,6 @@
     whole = pltpu.roll(whole * scale, lax.rem(256 - shift, 256), 1)
     dgrad_ref[...] = whole[0:9, 0:width]
 
-    gin_store.wait()
-    out_store.wait()
     for copies in (d_copies, c_copies, a_copies, w_copies, f_copies, r_copies, g_copies,
                    p_copies, q_copies):
         for copy in copies:
@@ -589,20 +582,17 @@
     dma = pltpu.SemaphoreType.DMA
     part = width // reps
     vmem = pl.BlockSpec(memory_space=pltpu.VMEM)
-    return pl.pallas_call(
+    results = pl.pallas_call(
         functools.partial(fused_kernel, n, reps, 1.0 / (n * reps)),
         out_shape=(
-            jax.ShapeDtypeStruct(latents.shape, bf),
-            jax.ShapeDtypeStruct(latents.shape, bf),
-            jax.ShapeDtypeStruct((9, width), f32),
-            jax.ShapeDtypeStruct((3, width, width), f32),
+            pltpu.VMEM(latents.shape, bf),
+            pltpu.VMEM(latents.shape, bf),
+            pltpu.VMEM((9, width), f32),
+            pltpu.VMEM((3, width, width), f32),
         ),
         in_specs=[pl.BlockSpec(memory_space=pltpu.HBM)] * 4,
-        out_specs=[pl.BlockSpec(memory_space=pltpu.HBM)] * 2 + [vmem] * 2,
+        out_specs=[vmem] * 4,
         scratch_shapes=[
-            pltpu.VMEM(latents.shape, bf),
-            pltpu.VMEM(latents.shape, bf),
-            dma((2,)),
             pltpu.VMEM(latents.shape, bf),
             pltpu.VMEM(depth_taps.shape, bf),
             pltpu.VMEM(time_taps.shape, bf),
@@ -645,9 +635,34 @@
             dma((reps - 1,)), dma((reps - 1,)),
         ],
         compiler_params=pltpu.CompilerParams(
-            collective_id=0, has_side_effects=True, vmem_limit_bytes=63 * 1024 * 1024
+            collective_id=0, has_side_effects=True, vmem_limit_bytes=24 * 1024 * 1024
         ),
-    )(latents, depth_taps, time_taps, cotangent)
+    )(*[pltpu.with_memory_space_constraint(a, pltpu.HBM)
+        for a in (latents, depth_taps, time_taps, cotangent)])
+    return store_out(results)
+
+
+def store_kernel(*refs):
+    sources, targets, sems = refs[:4], refs[4:8], refs[8]
+    copies = [
+        pltpu.make_async_copy(source, target, sems.at[i])
+        for i, (source, target) in enumerate(zip(sources, targets))
+    ]
+    for copy in copies:
+        copy.start()
+    for copy in copies:
+        copy.wait()
+
+
+def store_out(results):
+    return pl.pallas_call(
+        store_kernel,
+        out_shape=tuple(jax.ShapeDtypeStruct(r.shape, r.dtype) for r in results),
+        in_specs=[pl.BlockSpec(memory_space=pltpu.VMEM)] * 4,
+        out_specs=[pl.BlockSpec(memory_space=pltpu.HBM)] * 4,
+        scratch_shapes=[pltpu.SemaphoreType.DMA((4,))],
+        compiler_params=pltpu.CompilerParams(has_side_effects=True),
+    )(*[pltpu.with_memory_space_constraint(r, pltpu.VMEM) for r in results])
 
 
 def solution(mesh):

time: 39.5 us -> 35.8 us (0.906)
  local copies, waits for them, and re-layouts: 3.88 us -> 0 us
    unnamed x10 -> x0, local copies, waits for them, and re-layouts: 3.88 us -> none
    pallas_call x0 -> x1, Pallas kernels: none -> 1.04 us  [store_out(): pl.pallas_call(store_kernel, out_shape=tuple((jax.ShapeDtypeStruct(r.shap...]
    pallas_call x1, Pallas kernels: 34.7 us -> 33.9 us  [fused_device(): pl.pallas_call(functools.partial(fused_kernel, n, reps, 1.0 / (n * reps))...]
where the time goes in v1:
time: 35.8 us; the launch traced here: 35.6 us
  Pallas kernels  34.9 us (97%)
  between operations  0.64 us (2%)
    pallas_call x1, Pallas kernels, fused_device(): pl.pallas_call(functools.partial(fused_kernel, n, reps, 1.0 / (n * reps))...  33.9 us
    pallas_call x1, Pallas kernels, store_out(): pl.pallas_call(store_kernel, out_shape=tuple((jax.ShapeDtypeStruct(r.shap...  1.04 us

profile of v1, /device:TPU:0, one launch (start us, length us, event | category | flops | bytes accessed | tf_op | source)
XLA Modules:
  0.0 35.6 jit_solution(9593542065965324100)
XLA Ops:
  0.6 33.9 %shard_map.75 = (bf16[1,8,2,8,1280]{4,3,2,1,0:T(8,128)(2,1)S(1)}, bf16[1,8,2,8,1280]{4,3,2,1,0:T(8,128)(2,1)S(1)}, f32[9,160]{1,0:T(8,128)S(1)}, f32[3,160,160]{2,1,0:T(8,128)S(1)}) custom-call(bf16[1,8,2,8,1280]{4,3,2,1,0:T(8,128)(2,1)} %x_hbm.1, bf16[9,160]{1,0:T(8,128)(2,1)} %dtaps_hbm.1, bf16[3,160,160]{2,1,0:T(8,128)(2,1)} %ttaps_hbm.1, ...), custom_call_target="tpu_custom_call" | custom-call | tf_op jit(solution)/shard_map/pallas_call | solution.py:585
  34.5 1.0 %shard_map.76 = (bf16[1,8,2,8,1280]{4,3,2,1,0:T(8,128)(2,1)}, bf16[1,8,2,8,1280]{4,3,2,1,0:T(8,128)(2,1)}, f32[9,160]{1,0:T(8,128)}, f32[3,160,160]{2,1,0:T(8,128)}) custom-call(bf16[1,8,2,8,1280]{4,3,2,1,0:T(8,128)(2,1)S(1)} %get-tuple-element.8.refs_0_, bf16[1,8,2,8,1280]{4,3,2,1,0:T(8,128)(2,1)S(1)} %get-tuple-element.9.refs_1_, ...), custom_call_target="tpu_custom_call" | custom-call | tf_op jit(solution)/shard_map/pallas_call | solution.py:658

commit v2 on v1

v2 whole, which is shorter than its diff:
```python
import functools

import jax
import jax.numpy as jnp
from jax import lax
from jax.experimental import pallas as pl
from jax.experimental.pallas import tpu as pltpu
from jax.sharding import PartitionSpec as P

GROUPS = 8


def moved(field, offset):
    if offset == 0:
        return field
    filler = jnp.zeros((field.shape[0], abs(offset)), field.dtype)
    if offset > 0:
        return jnp.concatenate([field[:, offset:], filler], 1)
    return jnp.concatenate([filler, field[:, :offset]], 1)


def inside(frames, height, breadth, frame_off, row_off, col_off):
    places = jnp.arange(frames * height * breadth, dtype=jnp.int32)
    frame_at = places // (height * breadth) + frame_off
    row_at = places // breadth % height + row_off
    col_at = places % breadth + col_off
    valid = (frame_at >= 0) & (frame_at < frames) & (row_at >= 0) & (row_at < height)
    valid = valid & (col_at >= 0) & (col_at < breadth)
    return valid[None, :]


def clip_pass(latent, cotan, depth_full, time_full):
    frames, height, breadth, chans = latent.shape
    plane = height * breadth
    count = frames * plane
    width = chans // GROUPS
    x_cols = latent.reshape(count, chans).T
    dy_cols = cotan.reshape(count, chans).T
    wdf = depth_full.astype(jnp.float32)
    spatial = jnp.zeros((chans, count), jnp.float32)
    for tap in range(9):
        row_off = tap // 3 - 1
        col_off = tap % 3 - 1
        offset = row_off * breadth + col_off
        shifted = jnp.where(
            inside(frames, height, breadth, 0, row_off, col_off), moved(x_cols, offset), 0
        )
        spatial = spatial + shifted * wdf[tap][:, None]
    inv_rms = lax.rsqrt(jnp.mean(spatial * spatial, 0, keepdims=True) + 1e-05)
    normed = spatial * inv_rms
    activated = jax.nn.silu(normed).astype(jnp.bfloat16)
    act_parts = []
    dy_parts = []
    for step in range(3):
        act_off = step - 1
        act_shift = jnp.where(
            inside(frames, height, breadth, act_off, 0, 0), moved(activated, act_off * plane), 0
        )
        act_parts.append(act_shift.reshape(GROUPS, width, count))
        dy_off = 1 - step
        dy_shift = jnp.where(
            inside(frames, height, breadth, dy_off, 0, 0), moved(dy_cols, dy_off * plane), 0
        )
        dy_parts.append(dy_shift.reshape(GROUPS, width, count))
    act_stack = jnp.concatenate(act_parts, 1)
    dy_stack = jnp.concatenate(dy_parts, 1)
    grouped = time_full.reshape(3, width, GROUPS, width)
    fwd_weight = grouped.transpose(2, 3, 0, 1).reshape(GROUPS, width, 3 * width)
    back_weight = grouped.transpose(2, 1, 0, 3).reshape(GROUPS, width, 3 * width)
    temporal = jnp.einsum(
        "goc,gcr->gor", fwd_weight, act_stack, preferred_element_type=jnp.float32
    ).reshape(chans, count)
    block_out = (x_cols.astype(jnp.float32) + temporal).astype(jnp.bfloat16)
    act_grad = jnp.einsum(
        "gic,gcr->gir", back_weight, dy_stack, preferred_element_type=jnp.float32
    ).reshape(chans, count)
    dy_group = dy_cols.reshape(GROUPS, width, count)
    time_term = jnp.einsum("gcr,gor->goc", act_stack, dy_group, preferred_element_type=jnp.float32)
    time_term = (
        time_term.reshape(GROUPS, width, 3, width).transpose(2, 3, 0, 1).reshape(3, width, chans)
    )
    sig = jax.nn.sigmoid(normed)
    norm_grad = act_grad * sig * (1.0 + normed * (1.0 - sig))
    spatial_grad = inv_rms * (norm_grad - normed * jnp.mean(norm_grad * normed, 0, keepdims=True))
    input_grad = dy_cols.astype(jnp.float32)
    depth_terms = []
    for tap in range(9):
        row_off = tap // 3 - 1
        col_off = tap % 3 - 1
        offset = row_off * breadth + col_off
        back_shift = jnp.where(
            inside(frames, height, breadth, 0, -row_off, -col_off),
            moved(spatial_grad, -offset),
            0.0,
        )
        input_grad = input_grad + back_shift * wdf[tap][:, None]
        shifted = jnp.where(
            inside(frames, height, breadth, 0, row_off, col_off), moved(x_cols, offset), 0
        )
        depth_terms.append(jnp.sum(shifted.astype(jnp.float32) * spatial_grad, axis=1))
    depth_term = jnp.stack(depth_terms)
    out_rows = block_out.T.reshape(latent.shape)
    grad_rows = input_grad.astype(jnp.bfloat16).T.reshape(latent.shape)
    return (out_rows, grad_rows, depth_term, time_term)


def per_device(latents, depth_taps, time_taps, cotangent):
    depth_full, time_full = (
        lax.all_gather(depth_taps, "shard", axis=1, tiled=True),
        lax.all_gather(time_taps, "shard", axis=2, tiled=True),
    )
    block_out, input_grad, depth_term, time_term = clip_pass(
        latents[0], cotangent[0], depth_full, time_full
    )
    scale = jnp.float32(1.0 / (lax.axis_size("shard") * lax.axis_size("rep")))
    depth_term = depth_term * scale
    time_term = time_term * scale
    time_part, depth_part = (
        lax.psum_scatter(time_term, "shard", scatter_dimension=2, tiled=True),
        lax.psum_scatter(depth_term, "shard", scatter_dimension=1, tiled=True),
    )
    time_grad, depth_grad = lax.psum((time_part, depth_part), "rep")
    return (block_out[None], input_grad[None], depth_grad, time_grad)


MESH = pl.DeviceIdType.MESH
LANES = 128
PEERS = (1, 6, 2, 4, 7, 3, 5)
CHUNKS = 2


def window(group):
    return 128 * (group + group // 4)


def fused_kernel(
    n, reps, scale,
    x_hbm, dtaps_hbm, ttaps_hbm, dy_hbm,
    out_ref, gin_ref, dgrad_ref, tgrad_ref,
    x_ref, dtaps_ref, ttaps_ref, dy_ref, in_sem,
    sp, slope, ag, act_t, cot_t, act_all, cot_all, cot_sh,
    w_fwd, ret_send, ret_all, tem_send, tem_all,
    d_mine, d_all, d_full,
    tg, tg_send, tg_recv, tg_out, dg, dg_send, dg_recv, dz_mine, dz_recv,
    sent, d_rs, c_rs, a_rs, b_rs, t_rs, r_rs, g_rs, p_rs, q_rs,
):
    frames, height, breadth, chans = sp.shape
    plane = height * breadth
    count = frames * plane
    width = chans // n
    tiles = chans // LANES
    piece = width // CHUNKS
    me = lax.axis_index("shard")
    z = lax.axis_index("rep")
    shift = 32 * lax.rem(me, 4)
    turns = [1 - 2 * lax.rem(lax.div(me, 1 << b), 2) for b in range(3)]
    peers = {m: me + sum((1 << b) * turns[b] for b in range(3) if m >> b & 1) for m in PEERS}

    def zahead(r):
        return lax.rem(z + r, reps)

    def remote(src, dst, ss, rs, **where):
        return pltpu.make_async_remote_copy(
            src_ref=src, dst_ref=dst, send_sem=ss, recv_sem=rs,
            device_id=where, device_id_type=MESH,
        )

    def start(copies):
        for copy in copies:
            copy.start()

    def arrive(ref, sem):
        pltpu.make_async_copy(ref, ref, sem).wait()

    loads = [
        pltpu.make_async_copy(src, dst, in_sem.at[i])
        for i, (src, dst) in enumerate((
            (dtaps_hbm, dtaps_ref), (dy_hbm, dy_ref), (ttaps_hbm, ttaps_ref), (x_hbm, x_ref),
        ))
    ]
    for load in loads:
        load.start()
    barrier = pltpu.get_barrier_semaphore()
    for r in range(1, reps):
        pl.semaphore_signal(barrier, inc=1, device_id={"rep": zahead(r)}, device_id_type=MESH)
    for m in PEERS:
        pl.semaphore_signal(barrier, inc=1, device_id={"shard": peers[m]}, device_id_type=MESH)

    dg[...] = jnp.zeros(dg.shape, jnp.float32)
    cot_sh[3 * width:512, :] = jnp.zeros((512 - 3 * width, n * count), jnp.bfloat16)

    place = (
        lax.broadcasted_iota(jnp.int32, (width, 256), 1)
        == lax.broadcasted_iota(jnp.int32, (width, 256), 0) + shift
    ).astype(jnp.float32).astype(jnp.bfloat16)
    loads[0].wait()
    taps = jnp.concatenate(
        [dtaps_ref[...].astype(jnp.float32), jnp.zeros((7, width), jnp.float32)], axis=0
    ).astype(jnp.bfloat16)
    d_mine[...] = jnp.dot(taps, place, preferred_element_type=jnp.float32).astype(jnp.bfloat16)

    def cols_of(t):
        return pl.ds(pl.multiple_of(t * LANES, LANES), LANES)

    def cot_tile(t, carry):
        cols = cols_of(t)
        tile = dy_ref[0, :, :, :, cols].astype(jnp.float32).reshape(count, LANES)
        cot_t[cols, :] = tile.T.astype(jnp.bfloat16)
        return carry

    loads[1].wait()
    lax.fori_loop(0, tiles, cot_tile, 0, unroll=2)
    nt = (((1,), (1,)), ((), ()))
    loads[2].wait()
    same = (
        lax.broadcasted_iota(jnp.int32, (width, width), 0)
        == lax.broadcasted_iota(jnp.int32, (width, width), 1)
    ).astype(jnp.float32).astype(jnp.bfloat16)
    for k in range(3):
        w_fwd[k] = lax.dot_general(
            same, ttaps_ref[k], nt, preferred_element_type=jnp.float32
        ).astype(jnp.bfloat16)
    pl.semaphore_wait(barrier, n - 1 + reps - 1)

    def slab(p):
        return pl.ds(pl.multiple_of(p * width, 32), width)

    def d_copy(m, origin):
        return remote(d_mine, d_all.at[origin], sent.at[0], d_rs, shard=peers[m])

    def c_copy(m, origin):
        return remote(
            cot_t.at[slab(peers[m]), :], cot_all.at[origin],
            sent.at[1], c_rs.at[m // 2], shard=peers[m],
        )

    def a_copy(h, m, origin):
        rows = pl.ds(pl.multiple_of(peers[m] * width + piece * h, 16), piece)
        return remote(
            act_t.at[rows, :], act_all.at[origin, pl.ds(piece * h, piece)],
            sent.at[2], a_rs.at[h], shard=peers[m],
        )

    def b_copy(m, origin):
        return remote(
            ret_send.at[peers[m]], ret_all.at[slab(origin), :],
            sent.at[3], b_rs, shard=peers[m],
        )

    def t_copy(m, origin):
        return remote(
            tem_send.at[peers[m]], tem_all.at[slab(origin), :],
            sent.at[4], t_rs, shard=peers[m],
        )

    start([d_copy(m, me) for m in PEERS])
    start([c_copy(m, me) for m in PEERS])
    d_all[me] = d_mine[...]
    cot_all[me] = cot_t[slab(me), :]

    lane = lax.broadcasted_iota(jnp.int32, (width, count), 1)

    def later(v):
        return jnp.where(lane < count - plane, pltpu.roll(v, count - plane, 1), 0.0)

    def earlier(v):
        return jnp.where(lane >= plane, pltpu.roll(v, plane, 1), 0.0)

    def clipwise(step, v):
        clips = v.shape[1] // count
        return jnp.concatenate([step(v[:, i * count:(i + 1) * count]) for i in range(clips)], axis=1)

    def chip(p):
        return lax.div(p, 2) * 2

    def temporal(source, weights, first, clips, step, other, target):
        block = jnp.concatenate([source[first + i] for i in range(clips)], axis=1)
        terms = jnp.dot(
            weights[...].reshape(3 * width, width), block, preferred_element_type=jnp.float32
        )
        start_term, end_term = clipwise(step, terms[0:width]), clipwise(other, terms[2 * width:])
        total = (start_term + terms[width:2 * width] + end_term).astype(jnp.bfloat16)
        for i in range(clips):
            target[first + i] = total[:, i * count:(i + 1) * count]
        return block

    def back(first, clips):
        block = temporal(cot_all, ttaps_ref, first, clips, later, earlier, ret_send)
        lanes = pl.ds(pl.multiple_of(first * count, count * clips), count * clips)
        wide = block.astype(jnp.float32)
        cot_sh[0:width, lanes] = clipwise(later, wide).astype(jnp.bfloat16)
        cot_sh[width:2 * width, lanes] = block
        cot_sh[2 * width:3 * width, lanes] = clipwise(earlier, wide).astype(jnp.bfloat16)

    def forth(first):
        temporal(act_all, w_fwd, first, 2, earlier, later, tem_send)

    def give_back(*masks):
        clips = len(masks)
        first = peers[masks[0]] if clips == 1 else chip(peers[masks[0]])
        arrive(cot_all.at[pl.ds(first, clips)], c_rs.at[masks[0] // 2])
        back(first, clips)
        start([b_copy(m, me) for m in masks])

    back(me, 1)
    ret_all[slab(me), :] = ret_send[me]
    give_back(1)

    arrive(d_all.at[0:n - 1], d_rs)
    d_full[...] = jnp.zeros(d_full.shape, jnp.float32)
    for g in range(n):
        lo = window(g)
        d_full[:, lo:lo + 256] = d_full[:, lo:lo + 256] + d_all[g].astype(jnp.float32)

    column = lax.broadcasted_iota(jnp.int32, (frames, height, breadth, LANES), 2)

    def from_left(v):
        rolled = pltpu.roll(v.reshape(frames * height, breadth, LANES), 1, 1)
        return jnp.where(column == 0, 0.0, rolled.reshape(v.shape))

    def from_right(v):
        rolled = pltpu.roll(v.reshape(frames * height, breadth, LANES), breadth - 1, 1)
        return jnp.where(column == breadth - 1, 0.0, rolled.reshape(v.shape))

    def spatial_tile(t, carry):
        cols = cols_of(t)
        x = x_ref[0, :, :, :, cols].astype(jnp.float32)
        d = [d_full[k:k + 1, cols].reshape(1, 1, LANES) for k in range(9)]
        xs = [from_left(x), x, from_right(x)]
        top = sum(xs[j][:, 0] * d[3 + j] + xs[j][:, 1] * d[6 + j] for j in range(3))
        low = sum(xs[j][:, 0] * d[j] + xs[j][:, 1] * d[3 + j] for j in range(3))
        sp[:, 0, :, cols] = top
        sp[:, 1, :, cols] = low
        return (carry[0] + top * top, carry[1] + low * low)

    zero = jnp.zeros((frames, breadth, LANES), jnp.float32)
    loads[3].wait()
    squares = lax.fori_loop(0, tiles, spatial_tile, (zero, zero), unroll=2)
    inv = [
        lax.rsqrt(jnp.sum(s, axis=-1, keepdims=True) * (1.0 / chans) + 1e-05) for s in squares
    ]
    inv_rms = jnp.concatenate([v[:, None] for v in inv], axis=1)

    def act_tile(t, carry):
        cols = cols_of(t)
        normed = sp[:, :, :, cols] * inv_rms
        sig = jax.nn.sigmoid(normed)
        sp[:, :, :, cols] = normed
        slope[:, :, :, cols] = sig * (1.0 + normed * (1.0 - sig))
        tile = (normed * sig).reshape(count, LANES)
        act_t[cols, :] = tile.T.astype(jnp.bfloat16)
        return carry

    lax.fori_loop(0, tiles, act_tile, 0, unroll=2)
    for h in range(CHUNKS):
        start([a_copy(h, m, me) for m in PEERS])
    act_all[me] = act_t[slab(me), :]
    give_back(2, 3)
    give_back(4, 5)
    give_back(6, 7)

    def time_product(h):
        rows = slice(piece * h, piece * (h + 1))
        arrive(act_all.at[0:n - 1, rows], a_rs.at[h])
        acts = jnp.concatenate([act_all[p, rows] for p in range(n)], axis=1)
        product = lax.dot_general(acts, cot_sh[...], nt, preferred_element_type=jnp.float32)
        for q in range(reps):
            block = product[:, q * 512 // reps:(q + 1) * 512 // reps]
            tg[h, q] = block
            tg_send[h, q] = block.astype(jnp.bfloat16)
        start([
            remote(
                tg_send.at[h, zahead(r)], tg_recv.at[h, r - 1], sent.at[5], r_rs.at[h],
                rep=zahead(r),
            )
            for r in range(1, reps)
        ])

    def time_sum(h):
        arrive(tg_recv.at[h], r_rs.at[h])
        total = tg[h, z]
        for r in range(1, reps):
            total = total + tg_recv[h, r - 1].astype(jnp.float32)
        tg_out[h, z] = (total * scale).astype(jnp.bfloat16)
        start([
            remote(
                tg_out.at[h, z], tg_out.at[h, z], sent.at[6], g_rs.at[h], rep=zahead(r),
            )
            for r in range(1, reps)
        ])

    for h in range(CHUNKS):
        time_product(h)
    for m in (6, 2, 4):
        forth(chip(peers[m]))
        start([t_copy(m, me), t_copy(m + 1, me)])
    forth(chip(me))
    start([t_copy(1, me)])
    tem_all[slab(me), :] = tem_send[me]
    arrive(ret_all.at[0:(n - 1) * width, :], b_rs)

    def norm_tile(t, carry):
        cols = cols_of(t)
        back_rows = ret_all[cols, :].astype(jnp.float32).T
        grad = back_rows.reshape(frames, height, breadth, LANES) * slope[:, :, :, cols]
        ag[:, cols] = grad.reshape(count, LANES)
        return carry + grad * sp[:, :, :, cols]

    dots = lax.fori_loop(
        0, tiles, norm_tile, jnp.zeros((frames, height, breadth, LANES), jnp.float32), unroll=2)
    mean = jnp.sum(dots, axis=-1, keepdims=True) * (1.0 / chans)

    def depth_tile(t, carry):
        cols = cols_of(t)
        grad = ag[:, cols].reshape(frames, height, breadth, LANES)
        sg = inv_rms * (grad - sp[:, :, :, cols] * mean)
        ag[:, cols] = sg.reshape(count, LANES)
        gs = [from_right(sg), sg, from_left(sg)]
        x = x_ref[0, :, :, :, cols].astype(jnp.float32)
        x0, x1 = x[:, 0], x[:, 1]
        for j in range(3):
            g0, g1 = gs[j][:, 0], gs[j][:, 1]
            for i, term in enumerate((x0 * g1, x0 * g0 + x1 * g1, x1 * g0)):
                dg[3 * i + j:3 * i + j + 1, cols] = jnp.sum(
                    jnp.sum(term, axis=0), axis=0, keepdims=True
                )
        return carry

    lax.fori_loop(0, tiles, depth_tile, 0, unroll=2)

    def grad_tile(t, carry):
        cols = cols_of(t)
        sg = ag[:, cols].reshape(frames, height, breadth, LANES)
        d = [d_full[k:k + 1, cols].reshape(1, 1, LANES) for k in range(9)]
        gs = [from_right(sg), sg, from_left(sg)]
        top = dy_ref[0, :, 0, :, cols].astype(jnp.float32)
        low = dy_ref[0, :, 1, :, cols].astype(jnp.float32)
        for j in range(3):
            g0, g1 = gs[j][:, 0], gs[j][:, 1]
            top = top + g0 * d[3 + j] + g1 * d[j]
            low = low + g0 * d[6 + j] + g1 * d[3 + j]
        gin_ref[0, :, 0, :, cols] = top.astype(jnp.bfloat16)
        gin_ref[0, :, 1, :, cols] = low.astype(jnp.bfloat16)
        return carry

    def dwin(p):
        return pl.ds(pl.multiple_of(LANES * (p + lax.div(p, 4)), LANES), 256)

    def p_copy(m, origin):
        return remote(
            dg_send.at[:, dwin(peers[m])], dg_recv.at[origin], sent.at[7], p_rs, shard=peers[m],
        )

    dg_send[...] = dg[...].astype(jnp.bfloat16)
    start([p_copy(m, me) for m in PEERS])
    dg_recv[me] = dg_send[:, dwin(me)]

    time_sum(0)
    lax.fori_loop(0, tiles, grad_tile, 0, unroll=2)
    for h in range(1, CHUNKS):
        time_sum(h)
    arrive(dg_recv.at[0:n - 1], p_rs)
    total = dg_recv[0].astype(jnp.float32)
    for p in range(1, n):
        total = total + dg_recv[p].astype(jnp.float32)
    dz_mine[...] = total
    start([
        remote(dz_mine, dz_recv.at[z], sent.at[8], q_rs, rep=zahead(r))
        for r in range(1, reps)
    ])
    dz_recv[z] = dz_mine[...]

    arrive(tem_all.at[0:(n - 1) * width, :], t_rs)

    def out_tile(t, carry):
        cols = cols_of(t)
        x = x_ref[0, :, :, :, cols].astype(jnp.float32)
        moved_on = tem_all[cols, :].astype(jnp.float32).T
        y = x + moved_on.reshape(frames, height, breadth, LANES)
        out_ref[0, :, :, :, cols] = y.astype(jnp.bfloat16)
        return carry

    lax.fori_loop(0, tiles, out_tile, 0, unroll=2)

    for h in range(CHUNKS):
        arrive(tg_out.at[h, 0:reps - 1], g_rs.at[h])
        grads = jnp.concatenate([tg_out[h, q].astype(jnp.float32) for q in range(reps)], axis=1)
        for k in range(3):
            tgrad_ref[k, piece * h:piece * (h + 1), :] = grads[:, k * width:(k + 1) * width]

    arrive(dz_recv.at[0:reps - 1], q_rs)
    whole = dz_recv[0]
    for r in range(1, reps):
        whole = whole + dz_recv[r]
    whole = pltpu.roll(whole * scale, lax.rem(256 - shift, 256), 1)
    dgrad_ref[...] = whole[0:9, 0:width]

    shard_bytes = cot_t.at[0:(n - 1) * width, :]
    amounts = (
        d_all.at[0:n - 1], shard_bytes, shard_bytes, shard_bytes, shard_bytes,
        tg_recv, tg_recv, dg_recv.at[0:n - 1], dz_recv.at[0:reps - 1],
    )
    for i, amount in enumerate(amounts):
        arrive(amount, sent.at[i])


def fused_device(latents, depth_taps, time_taps, cotangent):
    n, reps = lax.axis_size("shard"), lax.axis_size("rep")
    _, frames, height, breadth, chans = latents.shape
    count = frames * height * breadth
    width = chans // n
    bf, f32 = jnp.bfloat16, jnp.float32
    dma = pltpu.SemaphoreType.DMA
    piece, part = width // CHUNKS, 512 // reps
    vmem = pl.BlockSpec(memory_space=pltpu.VMEM)
    results = pl.pallas_call(
        functools.partial(fused_kernel, n, reps, 1.0 / (n * reps)),
        out_shape=(
            pltpu.VMEM(latents.shape, bf),
            pltpu.VMEM(latents.shape, bf),
            pltpu.VMEM((9, width), f32),
            pltpu.VMEM((3, width, width), f32),
        ),
        in_specs=[pl.BlockSpec(memory_space=pltpu.HBM)] * 4,
        out_specs=[vmem] * 4,
        scratch_shapes=[
            pltpu.VMEM(latents.shape, bf),
            pltpu.VMEM(depth_taps.shape, bf),
            pltpu.VMEM(time_taps.shape, bf),
            pltpu.VMEM(cotangent.shape, bf),
            dma((4,)),
            pltpu.VMEM((frames, height, breadth, chans), f32),
            pltpu.VMEM((frames, height, breadth, chans), f32),
            pltpu.VMEM((count, chans), f32),
            pltpu.VMEM((chans, count), bf),
            pltpu.VMEM((chans, count), bf),
            pltpu.VMEM((n, width, count), bf),
            pltpu.VMEM((n, width, count), bf),
            pltpu.VMEM((512, n * count), bf),
            pltpu.VMEM((3, width, width), bf),
            pltpu.VMEM((n, width, count), bf),
            pltpu.VMEM((chans, count), bf),
            pltpu.VMEM((n, width, count), bf),
            pltpu.VMEM((chans, count), bf),
            pltpu.VMEM((16, 256), bf),
            pltpu.VMEM((n, 16, 256), bf),
            pltpu.VMEM((16, chans), f32),
            pltpu.VMEM((CHUNKS, reps, piece, part), f32),
            pltpu.VMEM((CHUNKS, reps, piece, part), bf),
            pltpu.VMEM((CHUNKS, reps - 1, piece, part), bf),
            pltpu.VMEM((CHUNKS, reps, piece, part), bf),
            pltpu.VMEM((16, chans), f32),
            pltpu.VMEM((16, chans), bf),
            pltpu.VMEM((n, 16, 256), bf),
            pltpu.VMEM((16, 256), f32),
            pltpu.VMEM((reps, 16, 256), f32),
            dma((9,)), dma, dma((n // 2,)), dma((CHUNKS,)), dma, dma,
            dma((CHUNKS,)), dma((CHUNKS,)), dma, dma,
        ],
        compiler_params=pltpu.CompilerParams(
            collective_id=0, has_side_effects=True, vmem_limit_bytes=24 * 1024 * 1024
        ),
    )(*[pltpu.with_memory_space_constraint(a, pltpu.HBM)
        for a in (latents, depth_taps, time_taps, cotangent)])
    return store_out(results)


def store_kernel(*refs):
    sources, targets, sems = refs[:4], refs[4:8], refs[8]
    copies = [
        pltpu.make_async_copy(source, target, sems.at[i])
        for i, (source, target) in enumerate(zip(sources, targets))
    ]
    for copy in copies:
        copy.start()
    for copy in copies:
        copy.wait()


def store_out(results):
    return pl.pallas_call(
        store_kernel,
        out_shape=tuple(jax.ShapeDtypeStruct(r.shape, r.dtype) for r in results),
        in_specs=[pl.BlockSpec(memory_space=pltpu.VMEM)] * 4,
        out_specs=[pl.BlockSpec(memory_space=pltpu.HBM)] * 4,
        scratch_shapes=[pltpu.SemaphoreType.DMA((4,))],
        compiler_params=pltpu.CompilerParams(has_side_effects=True),
    )(*[pltpu.with_memory_space_constraint(r, pltpu.VMEM) for r in results])


def solution(mesh):
    placed = (
        P(("shard", "rep"), None, None, None, None),
        P(None, "shard"),
        P(None, None, "shard"),
        P(("shard", "rep"), None, None, None, None),
    )
    shards, reps = mesh.shape["shard"], mesh.shape["rep"]
    fused = shards == GROUPS and reps in (2, 4)
    return jax.shard_map(
        fused_device if fused else per_device,
        mesh=mesh,
        in_specs=placed,
        out_specs=(
            P(("shard", "rep"), None, None, None, None),
            P(("shard", "rep"), None, None, None, None),
            P(None, "shard"),
            P(None, None, "shard"),
        ),
        check_vma=False,
    )
```

time: 35.8 us -> 30.8 us (0.86)
  Pallas kernels: 34.9 us -> 30 us
    pallas_call x1, Pallas kernels: 33.9 us -> 28.9 us  [fused_device(): pl.pallas_call(functools.partial(fused_kernel, n, reps, 1.0 / (n * reps))...]
where the time goes in v2:
time: 30.8 us; the launch traced here: 30.6 us
  Pallas kernels  30 us (97%)
  between operations  0.64 us (2%)
    pallas_call x1, Pallas kernels, fused_device(): pl.pallas_call(functools.partial(fused_kernel, n, reps, 1.0 / (n * reps))...  28.9 us
    pallas_call x1, Pallas kernels, store_out(): pl.pallas_call(store_kernel, out_shape=tuple((jax.ShapeDtypeStruct(r.shap...  1.04 us

profile of v2, /device:TPU:0, one launch (start us, length us, event | category | flops | bytes accessed | tf_op | source)
XLA Modules:
  0.0 30.6 jit_solution(14342779019328891246)
XLA Ops:
  0.6 28.9 %shard_map.75 = (bf16[1,8,2,8,1280]{4,3,2,1,0:T(8,128)(2,1)S(1)}, bf16[1,8,2,8,1280]{4,3,2,1,0:T(8,128)(2,1)S(1)}, f32[9,160]{1,0:T(8,128)S(1)}, f32[3,160,160]{2,1,0:T(8,128)S(1)}) custom-call(bf16[1,8,2,8,1280]{4,3,2,1,0:T(8,128)(2,1)} %x_hbm.1, bf16[9,160]{1,0:T(8,128)(2,1)} %dtaps_hbm.1, bf16[3,160,160]{2,1,0:T(8,128)(2,1)} %ttaps_hbm.1, ...), custom_call_target="tpu_custom_call" | custom-call | tf_op jit(solution)/shard_map/pallas_call | solution.py:516
  29.6 1.0 %shard_map.76 = (bf16[1,8,2,8,1280]{4,3,2,1,0:T(8,128)(2,1)}, bf16[1,8,2,8,1280]{4,3,2,1,0:T(8,128)(2,1)}, f32[9,160]{1,0:T(8,128)}, f32[3,160,160]{2,1,0:T(8,128)}) custom-call(bf16[1,8,2,8,1280]{4,3,2,1,0:T(8,128)(2,1)S(1)} %get-tuple-element.8.refs_0_, bf16[1,8,2,8,1280]{4,3,2,1,0:T(8,128)(2,1)S(1)} %get-tuple-element.9.refs_1_, ...), custom_call_target="tpu_custom_call" | custom-call | tf_op jit(solution)/shard_map/pallas_call | solution.py:581
